TPU v7x, 512 devices: a whole 4x4x16 slice. The times are simulated.
512 devices in a mesh: tm: 8 (over x, core), dp: 64 (over z, y).
Axes of the slice: x: 4, y: 4, z: 16, core: 2. Of those that a mesh axis runs over, the one named last changes fastest.
Arguments:
- edge_feat: bfloat16 [8, 8192, 186], P('tm', 'dp'), may hold values from -6 to 6
- endpoint_slots: int32 [8, 2, 8192], P('tm', None, 'dp'), may hold values from 0 to 2047, as said below
- neighbor_slots: int32 [8, 20, 8192], P('tm', None, 'dp'), may hold values from 0 to 2047, as said below
- neighbor_gap: int32 [8, 20, 8192], P('tm', None, 'dp'), may hold values from 0 to 999
- score_grad: float32 [8, 8192], P('tm', 'dp'), may hold values from -1.5 to 1.5
- node_list: int32 [8, 64, 2048], P('tm', 'dp'), may hold values from 0 to 128, as said below
- memory0: float32 [8192, 256], P('dp'), may hold values from -6 to 6
- msg_weight: bfloat16 [186, 256], replicated, may hold values from -0.4375 to 0.4375
- gate_weight: bfloat16 [256, 512], replicated, may hold values from -0.375 to 0.375
- gate_bias: float32 [512], replicated, may hold values from -4 to 4
- omega: float32 [256], replicated, may hold values from 0.001 to 1
- attn_weights: bfloat16 [4, 256, 256], replicated, may hold values from -0.375 to 0.375
- pred_weights: bfloat16 [2, 256, 256], replicated, may hold values from -0.375 to 0.375
- pred_out: float32 [256], replicated, may hold values from -0.375 to 0.375
Outputs:
- scores: float32 [8, 8192], P('tm', 'dp')
- new_memory: float32 [8, 8192, 256], P('tm', 'dp')
- grad_out_proj: float32 [256, 256], replicated
- grad_pred: float32 [2, 256, 256], replicated
Inputs may be any that keep to these rules, and one draw needn't show every extreme that they name: `node_list`: each block of 32 slots (one device's requests to one owner) holds distinct rows first and 128 in the empty slots after them; every block holds at least one row; in each mini-batch some owner's block is full from every device. `endpoint_slots`: every slot points at a non-empty entry of its device's node list. `neighbor_slots`: every slot points at a non-empty entry of its device's node list.
All inputs are finite; a program needn't handle non-finite values.
Results may differ from a plain program's by a relative error of at most 0.017.
Values may be sent and summed in bfloat16 or wider, within the bound.
No kernel may reach another device: no remote copies, remote signals or barrier semaphores. Data moves between devices by JAX's collectives and lax.ppermute only.
A program may use at most 64 MiB of HBM per device.

v0:
```python
import math
import jax
import jax.numpy as jnp
from jax import lax
from jax.sharding import PartitionSpec as P

HEADS = 2


def local_step(
    slot_rows,
    end_slots,
    near_slots,
    near_gaps,
    cot_rows,
    omega,
    attn_weights,
    pred_weights,
    pred_out,
):
    feat_width = slot_rows.shape[1]
    events = end_slots.shape[1]
    near_count = near_slots.shape[0] // 2
    head_dim = feat_width // HEADS
    self_rows = jnp.take(slot_rows, end_slots, axis=0)
    near_rows = jnp.take(slot_rows, near_slots, axis=0).reshape(2, near_count, events, feat_width)
    phases = near_gaps.reshape(2, near_count, events).astype(jnp.float32)[..., None] * omega
    near_feat = (near_rows.astype(jnp.float32) + jnp.cos(phases)).astype(jnp.bfloat16)
    query_proj = jnp.einsum(
        "pea,ab->peb", self_rows, attn_weights[0], preferred_element_type=jnp.float32
    )
    key_proj = jnp.einsum(
        "pkea,ab->pkeb", near_feat, attn_weights[1], preferred_element_type=jnp.float32
    )
    value_proj = jnp.einsum(
        "pkea,ab->pkeb", near_feat, attn_weights[2], preferred_element_type=jnp.float32
    )
    query_heads = query_proj.reshape(2, 1, events, HEADS, head_dim)
    key_heads = key_proj.reshape(2, near_count, events, HEADS, head_dim)
    value_heads = value_proj.reshape(2, near_count, events, HEADS, head_dim)
    att_logits = jnp.sum(query_heads * key_heads, axis=-1) / math.sqrt(head_dim)
    weights_att = jax.nn.softmax(att_logits, axis=1)
    mixed_heads = (
        jnp.sum(weights_att[..., None] * value_heads, axis=1)
        .reshape(2, events, feat_width)
        .astype(jnp.bfloat16)
    )
    state_full = self_rows.astype(jnp.float32) + jnp.einsum(
        "pea,ab->peb", mixed_heads, attn_weights[3], preferred_element_type=jnp.float32
    )
    state_bf = state_full.astype(jnp.bfloat16)
    pre_pred = jnp.dot(state_bf[0], pred_weights[0], preferred_element_type=jnp.float32) + jnp.dot(
        state_bf[1], pred_weights[1], preferred_element_type=jnp.float32
    )
    sigmoid_pre = jax.nn.sigmoid(pre_pred)
    logit_out = jnp.sum(pre_pred * sigmoid_pre * pred_out, axis=-1)
    grad_pre = (
        cot_rows[:, None] * pred_out * (sigmoid_pre * (1.0 + pre_pred * (1.0 - sigmoid_pre)))
    ).astype(jnp.bfloat16)
    grad_first = jnp.einsum("ea,eb->ab", state_bf[0], grad_pre, preferred_element_type=jnp.float32)
    grad_second = jnp.einsum("ea,eb->ab", state_bf[1], grad_pre, preferred_element_type=jnp.float32)
    grad_state = jnp.einsum(
        "eb,pab->pea", grad_pre, pred_weights, preferred_element_type=jnp.float32
    ).astype(jnp.bfloat16)
    grad_out_proj = jnp.einsum(
        "pea,peb->ab", mixed_heads, grad_state, preferred_element_type=jnp.float32
    )
    return (logit_out, grad_out_proj, jnp.stack([grad_first, grad_second]))


def exchange(value, axis):
    return lax.all_to_all(value, axis, split_axis=0, concat_axis=0, tiled=True)


def sum_everywhere(grads):
    parts, spots = (lax.axis_size("tm"), lax.axis_size("dp"))
    rows, width = grads.shape
    own = rows // parts
    pieces = exchange(grads.astype(jnp.bfloat16).reshape(parts, own, width), "tm")
    mine = jnp.sum(pieces.astype(jnp.float32), axis=0).astype(jnp.bfloat16)
    cells = own * width // spots // 128
    pieces = exchange(mine.reshape(spots, cells, 128), "dp")
    mine = jnp.sum(pieces.astype(jnp.float32), axis=0).astype(jnp.bfloat16)
    whole = exchange(jnp.broadcast_to(mine[None], (spots, cells, 128)), "dp")
    whole = whole.reshape(own, width)
    return lax.all_gather(whole, "tm", axis=0, tiled=True).astype(jnp.float32)


def per_device(
    edge_feat,
    endpoint_slots,
    neighbor_slots,
    neighbor_gap,
    score_grad,
    node_list,
    memory0,
    msg_weight,
    gate_weight,
    gate_bias,
    omega,
    attn_weights,
    pred_weights,
    pred_out,
):
    groups = lax.axis_size("dp")
    batches = lax.axis_size("tm")
    node_dev, feat_width = memory0.shape
    list_len = node_list.shape[2]
    per_owner = list_len // groups
    requests = node_list[0, 0].reshape(groups, per_owner)
    message = jnp.dot(edge_feat[0], msg_weight, preferred_element_type=jnp.float32).astype(
        jnp.bfloat16
    )
    end_slots = endpoint_slots[0]
    slot_of = jnp.arange(list_len, dtype=jnp.int32)[:, None]
    hits = (end_slots[0][None, :] == slot_of).astype(jnp.float32) + (
        end_slots[1][None, :] == slot_of
    ).astype(jnp.float32)
    slot_tally = jnp.sum(hits, axis=1).astype(jnp.int32)
    slot_sums = jnp.dot(
        hits.astype(jnp.bfloat16), message, preferred_element_type=jnp.float32
    ).astype(jnp.bfloat16)
    small = exchange(
        jnp.concatenate([requests, slot_tally.reshape(groups, per_owner)], axis=1), "dp"
    )
    got_sums = exchange(slot_sums.reshape(groups, per_owner, feat_width), "dp")
    wanted = small[:, :per_owner].reshape(-1)
    got_tally = small[:, per_owner:].reshape(-1)
    picker = (wanted[:, None] == jnp.arange(node_dev)[None, :]).astype(jnp.bfloat16)
    totals = jnp.einsum(
        "sn,sd->nd", picker, got_sums.reshape(-1, feat_width), preferred_element_type=jnp.float32
    )
    counts = jnp.sum(
        jnp.where(wanted[:, None] == jnp.arange(node_dev)[None, :], got_tally[:, None], 0), axis=0
    ).astype(jnp.float32)
    touched = (counts > 0.5).astype(jnp.float32)
    mean_msg = (totals / jnp.maximum(counts, 1.0)[:, None]).astype(jnp.bfloat16)
    pre_gate = jnp.dot(mean_msg, gate_weight, preferred_element_type=jnp.float32) + gate_bias
    update = jax.nn.sigmoid(pre_gate[:, :feat_width]) * touched[:, None]
    candidate = jnp.tanh(pre_gate[:, feat_width:])
    decay_rate = 1.0 - update
    inject = update * candidate
    section_index = lax.axis_index("tm")
    share = node_dev // batches
    steps = exchange(
        jnp.concatenate(
            [
                decay_rate.astype(jnp.bfloat16).reshape(batches, share, feat_width),
                inject.astype(jnp.bfloat16).reshape(batches, share, feat_width),
            ],
            axis=1,
        ),
        "tm",
    ).astype(jnp.float32)
    state = lax.dynamic_slice_in_dim(memory0, section_index * share, share, axis=0)
    states = []
    for batch in range(batches):
        states.append(state.astype(jnp.bfloat16))
        state = steps[batch, :share] * state + steps[batch, share:]
    memory_bf = exchange(jnp.stack(states), "tm").reshape(node_dev, feat_width)
    before = jnp.where(section_index == 0, memory0, memory_bf.astype(jnp.float32))
    new_memory = decay_rate * before + inject
    sent_rows = jnp.dot(picker, memory_bf, preferred_element_type=jnp.float32).astype(jnp.bfloat16)
    slot_rows = exchange(sent_rows.reshape(groups, per_owner, feat_width), "dp").reshape(
        list_len, feat_width
    )
    logit_out, grad_out, grad_pair = local_step(
        slot_rows,
        end_slots,
        neighbor_slots[0],
        neighbor_gap[0],
        score_grad[0],
        omega,
        attn_weights,
        pred_weights,
        pred_out,
    )
    grads = sum_everywhere(jnp.concatenate([grad_out[None], grad_pair]).reshape(-1, feat_width))
    grads = grads.reshape(3, feat_width, feat_width)
    return (logit_out[None, :], new_memory[None], grads[0], grads[1:])


def solution(mesh):
    in_specs = (
        P("tm", "dp", None),
        P("tm", None, "dp"),
        P("tm", None, "dp"),
        P("tm", None, "dp"),
        P("tm", "dp"),
        P("tm", "dp", None),
        P("dp", None),
        P(),
        P(),
        P(),
        P(),
        P(),
        P(),
        P(),
    )
    out_specs = (P("tm", "dp"), P("tm", "dp", None), P(), P())
    return jax.shard_map(
        per_device, mesh=mesh, in_specs=in_specs, out_specs=out_specs, check_vma=False
    )
```

profile of v0, /device:TPU:1, one launch (start us, length us, event | category | flops | bytes accessed | tf_op | source)
XLA Modules:
  0.0 273.3 jit_solution(15879573352199052210)
XLA Ops:
  2.4 1.4 reduce.7
  4.5 19.3 %all-to-all-start = ((s32[64,1,64]{2,1,0:T(1,128)}), s32[64,1,64]{2,1,0:T(1,128)S(1)}, u32[]{:S(2)}, u32[]{:S(2)}) async-start(s32[64,1,64]{2,1,0:T(1,128)} %bitcast.4), calls=%async_computation | async-start | bytes 65536 | tf_op jit(solution)/shard_map/all_to_all | solution.py:72
  23.8 2.6 convolution_convert_fusion
  26.3 10.8 %all-to-all-done = s32[64,1,64]{2,1,0:T(1,128)S(1)} async-done(((s32[64,1,64]{2,1,0:T(1,128)}), s32[64,1,64]{2,1,0:T(1,128)S(1)}, u32[]{:S(2)}, u32[]{:S(2)}) %all-to-all-start) | async-done | bytes 16416 | tf_op jit(solution)/shard_map/all_to_all | solution.py:72
  37.2 4.7 %all-to-all-start.1 = ((bf16[64,32,256]{2,1,0:T(8,128)(2,1)}), bf16[64,32,256]{2,1,0:T(8,128)(2,1)S(1)}, u32[]{:S(2)}, u32[]{:S(2)}) async-start(bf16[64,32,256]{2,1,0:T(8,128)(2,1)} %bitcast.8), calls=%async_computation.1 | async-start | bytes 2097152 | tf_op jit(solution)/shard_map/all_to_all | solution.py:72
  42.0 1.2 select_reduce_fusion
  43.3 48.9 %all-to-all-done.1 = bf16[64,32,256]{2,1,0:T(8,128)(2,1)S(1)} async-done(((bf16[64,32,256]{2,1,0:T(8,128)(2,1)}), bf16[64,32,256]{2,1,0:T(8,128)(2,1)S(1)}, u32[]{:S(2)}, u32[]{:S(2)}) %all-to-all-start.1) | async-done | bytes 1048608 | tf_op jit(solution)/shard_map/all_to_all | solution.py:72
  93.8 10.3 %all-to-all-start.2 = ((bf16[8,32,256]{2,1,0:T(8,128)(2,1)}), bf16[8,32,256]{2,1,0:T(8,128)(2,1)S(1)}, u32[]{:S(2)}, u32[]{:S(2)}) async-start(bf16[8,32,256]{2,1,0:T(8,128)(2,1)} %pad_maximum_fusion.1), calls=%async_computation.2 | async-start | bytes 262144 | tf_op jit(solution)/shard_map/all_to_all | solution.py:72
  104.1 5.3 %all-to-all-done.2 = bf16[8,32,256]{2,1,0:T(8,128)(2,1)S(1)} async-done(((bf16[8,32,256]{2,1,0:T(8,128)(2,1)}), bf16[8,32,256]{2,1,0:T(8,128)(2,1)S(1)}, u32[]{:S(2)}, u32[]{:S(2)}) %all-to-all-start.2) | async-done | bytes 131104 | tf_op jit(solution)/shard_map/all_to_all | solution.py:72
  109.5 8.1 %all_to_all.47 = bf16[8,16,256]{2,1,0:T(8,128)(2,1)S(1)} all-to-all(bf16[8,16,256]{2,1,0:T(8,128)(2,1)S(1)} %constant_dynamic-update-slice_fusion), channel_id=1, replica_groups=mesh['tm'=8,'dp'=64] {'tm'}, dimensions={0} | all-to-all | bytes 131072 | tf_op jit(solution)/shard_map/all_to_all | solution.py:72
  117.6 1.5 convolution_convert_fusion.1
  119.1 5.7 %all-to-all-start.4 = ((bf16[64,32,256]{2,1,0:T(8,128)(2,1)}), bf16[64,32,256]{2,1,0:T(8,128)(2,1)S(1)}, u32[]{:S(2)}, u32[]{:S(2)}) async-start(bf16[64,32,256]{2,1,0:T(8,128)(2,1)} %bitcast.34), calls=%async_computation.4 | async-start | bytes 2097152 | tf_op jit(solution)/shard_map/all_to_all | solution.py:72
  126.0 50.3 %all-to-all-done.4 = bf16[64,32,256]{2,1,0:T(8,128)(2,1)S(1)} async-done(((bf16[64,32,256]{2,1,0:T(8,128)(2,1)}), bf16[64,32,256]{2,1,0:T(8,128)(2,1)S(1)}, u32[]{:S(2)}, u32[]{:S(2)}) %all-to-all-start.4) | async-done | bytes 1048608 | tf_op jit(solution)/shard_map/all_to_all | solution.py:72
  176.3 1.2 gather_fusion
  177.4 7.6 %gather_fusion.1 = bf16[2560,256]{1,0:T(8,128)(2,1)S(1)} fusion(bf16[2048,256]{1,0:T(8,128)(2,1)S(1)} %bitcast.271, s32[3072]{0:T(1024)S(1)} %pad_clamp_fusion), kind=kCustom, calls=%fused_computation.1 | custom fusion | bytes 2631680 | tf_op jit(solution)/shard_map/jit(_take)/gather | solution.py:26
  185.3 10.1 %add_convert_fusion = bf16[20,128,256]{2,1,0:T(8,128)(2,1)S(1)} fusion(f32[256]{0:T(256)S(1)} %copy-done.8, f32[20,128]{1,0:T(8,128)S(1)} %bitcast.289, bf16[20,128,256]{2,1,0:T(8,128)(2,1)S(1)} %bitcast.272, pred[20,128]{1,0:T(8,128)(4,1)S(1)} %compare_and_fusion), kind=kLoop, calls=%fused_computation.4 | loop fusion | flops 3276800 | bytes 2635264 | tf_op jit(solution)/shard_map/convert_element_type | solution.py:28
  196.2 1.1 multiply_reduce_fusion
  197.4 1.1 fusion.1
  200.4 15.2 %all_to_all.48 = bf16[8,96,256]{2,1,0:T(8,128)(2,1)S(1)} all-to-all(bf16[8,96,256]{2,1,0:T(8,128)(2,1)S(1)} %bitcast.273), channel_id=1, replica_groups=mesh['tm'=8,'dp'=64] {'tm'}, dimensions={0} | all-to-all | bytes 786432 | tf_op jit(solution)/shard_map/all_to_all | solution.py:72
  216.4 5.6 %all-to-all-start.6 = ((bf16[64,3,128]{2,1,0:T(4,128)(2,1)}), bf16[64,3,128]{2,1,0:T(4,128)(2,1)S(1)}, u32[]{:S(2)}, u32[]{:S(2)}) async-start(bf16[64,3,128]{2,1,0:T(4,128)(2,1)} %reshape.230), calls=%async_computation.6 | async-start | bytes 131072 | tf_op jit(solution)/shard_map/all_to_all | solution.py:72
  222.0 14.0 %all-to-all-done.6 = bf16[64,3,128]{2,1,0:T(4,128)(2,1)S(1)} async-done(((bf16[64,3,128]{2,1,0:T(4,128)(2,1)}), bf16[64,3,128]{2,1,0:T(4,128)(2,1)S(1)}, u32[]{:S(2)}, u32[]{:S(2)}) %all-to-all-start.6) | async-done | bytes 49184 | tf_op jit(solution)/shard_map/all_to_all | solution.py:72
  236.7 4.6 %all-to-all-start.7 = ((bf16[64,3,128]{2,1,0:T(4,128)(2,1)}), bf16[64,3,128]{2,1,0:T(4,128)(2,1)S(1)}, u32[]{:S(2)}, u32[]{:S(2)}) async-start(bf16[64,3,128]{2,1,0:T(4,128)(2,1)} %broadcast_in_dim.73), calls=%async_computation.7 | async-start | bytes 131072 | tf_op jit(solution)/shard_map/all_to_all | solution.py:72
  242.1 13.3 %all-to-all-done.7 = bf16[64,3,128]{2,1,0:T(4,128)(2,1)S(1)} async-done(((bf16[64,3,128]{2,1,0:T(4,128)(2,1)}), bf16[64,3,128]{2,1,0:T(4,128)(2,1)S(1)}, u32[]{:S(2)}, u32[]{:S(2)}) %all-to-all-start.7) | async-done | bytes 49184 | tf_op jit(solution)/shard_map/all_to_all | solution.py:72
  255.4 16.4 %all_gather.3 = bf16[768,256]{1,0:T(8,128)(2,1)S(1)} all-gather(bf16[96,256]{1,0:T(8,128)(2,1)S(1)} %reshape.231), channel_id=1, replica_groups=mesh['tm'=8,'dp'=64] {'tm'}, dimensions={0}, use_global_device_ids=true | all-gather | bytes 442368 | tf_op jit(solution)/shard_map/all_gather | solution.py:86
  (80 shorter events, 12.4 us)
Async XLA Ops:
  0.6 91.5 %copy-start = (bf16[256,512]{1,0:T(8,128)(2,1)S(1)}, bf16[256,512]{1,0:T(8,128)(2,1)}, u32[]{:S(2)}) copy-start(bf16[256,512]{1,0:T(8,128)(2,1)} %param.22) | copy-start | bytes 786436
  4.5 32.7 %all-to-all-start = ((s32[64,1,64]{2,1,0:T(1,128)}), s32[64,1,64]{2,1,0:T(1,128)S(1)}, u32[]{:S(2)}, u32[]{:S(2)}) async-start(s32[64,1,64]{2,1,0:T(1,128)} %bitcast.4), calls=%async_computation | async-start | bytes 65536 | tf_op jit(solution)/shard_map/all_to_all | solution.py:72
  26.3 65.8 %copy-start.9 = (f32[512]{0:T(512)S(1)}, f32[512]{0:T(512)}, u32[]{:S(2)}) copy-start(f32[512]{0:T(512)} %param.23) | copy-start | bytes 6148
  37.2 54.9 %all-to-all-start.1 = ((bf16[64,32,256]{2,1,0:T(8,128)(2,1)}), bf16[64,32,256]{2,1,0:T(8,128)(2,1)S(1)}, u32[]{:S(2)}, u32[]{:S(2)}) async-start(bf16[64,32,256]{2,1,0:T(8,128)(2,1)} %bitcast.8), calls=%async_computation.1 | async-start | bytes 2097152 | tf_op jit(solution)/shard_map/all_to_all | solution.py:72
  92.1 12.0 %copy-start.3 = (f32[128,256]{1,0:T(8,128)S(1)}, f32[128,256]{1,0:T(8,128)}, u32[]{:S(2)}) copy-start(f32[128,256]{1,0:T(8,128)} %param.20) | copy-start | bytes 393220
  93.8 15.5 %all-to-all-start.2 = ((bf16[8,32,256]{2,1,0:T(8,128)(2,1)}), bf16[8,32,256]{2,1,0:T(8,128)(2,1)S(1)}, u32[]{:S(2)}, u32[]{:S(2)}) async-start(bf16[8,32,256]{2,1,0:T(8,128)(2,1)} %pad_maximum_fusion.1), calls=%async_computation.2 | async-start | bytes 262144 | tf_op jit(solution)/shard_map/all_to_all | solution.py:72
  119.1 5.7 %copy-start.6 = (s32[1,20,128]{2,0,1:T(1,128)S(1)}, s32[1,20,128]{2,0,1:T(1,128)}, u32[]{:S(2)}) copy-start(s32[1,20,128]{2,0,1:T(1,128)} %param.17) | copy-start | bytes 30724
  119.1 5.8 %copy-start.2 = (bf16[4,256,256]{2,1,0:T(8,128)(2,1)S(1)}, bf16[4,256,256]{2,1,0:T(8,128)(2,1)}, u32[]{:S(2)}) copy-start(bf16[4,256,256]{2,1,0:T(8,128)(2,1)} %param.25) | copy-start | bytes 1572868
  119.1 57.2 %all-to-all-start.4 = ((bf16[64,32,256]{2,1,0:T(8,128)(2,1)}), bf16[64,32,256]{2,1,0:T(8,128)(2,1)S(1)}, u32[]{:S(2)}, u32[]{:S(2)}) async-start(bf16[64,32,256]{2,1,0:T(8,128)(2,1)} %bitcast.34), calls=%async_computation.4 | async-start | bytes 2097152 | tf_op jit(solution)/shard_map/all_to_all | solution.py:72
  124.8 1.1 copy-start.7
  124.8 1.1 copy-start.5
  177.4 7.9 %copy-start.8 = (f32[256]{0:T(256)S(1)}, f32[256]{0:T(256)}, u32[]{:S(2)}) copy-start(f32[256]{0:T(256)} %param.24) | copy-start | bytes 3076
  185.3 10.1 %copy-start.4 = (bf16[256,256]{1,0:T(8,128)(2,1)S(1)}, bf16[256,256]{1,0:T(8,128)(2,1)}, u32[]{:S(2)}) copy-start(bf16[256,256]{1,0:T(8,128)(2,1)} %copy.44) | copy-start | bytes 393220
  196.1 2.4 copy-start.1
  196.1 2.6 copy-start.10
  196.1 2.6 copy-start.11
  216.4 19.6 %all-to-all-start.6 = ((bf16[64,3,128]{2,1,0:T(4,128)(2,1)}), bf16[64,3,128]{2,1,0:T(4,128)(2,1)S(1)}, u32[]{:S(2)}, u32[]{:S(2)}) async-start(bf16[64,3,128]{2,1,0:T(4,128)(2,1)} %reshape.230), calls=%async_computation.6 | async-start | bytes 131072 | tf_op jit(solution)/shard_map/all_to_all | solution.py:72
  236.7 18.6 %all-to-all-start.7 = ((bf16[64,3,128]{2,1,0:T(4,128)(2,1)}), bf16[64,3,128]{2,1,0:T(4,128)(2,1)S(1)}, u32[]{:S(2)}, u32[]{:S(2)}) async-start(bf16[64,3,128]{2,1,0:T(4,128)(2,1)} %broadcast_in_dim.73), calls=%async_computation.7 | async-start | bytes 131072 | tf_op jit(solution)/shard_map/all_to_all | solution.py:72
where the time goes:
time: 274 us; the launch traced here: 273 us
  waiting for transfers between devices  142 us (52%)
  starting transfers between devices  50.1 us (18%)
  blocking collectives  39.7 us (14%)
  other arithmetic  15.7 us (6%)
  local copies, waits for them, and re-layouts  14.5 us (5%)
  matrix products  9.86 us (4%)
    all_to_all x6, waiting for transfers between devices, exchange(): return lax.all_to_all(value, axis, split_axis=0, concat_axis=0, tiled=True)  142 us
    all_to_all x6, starting transfers between devices, exchange(): return lax.all_to_all(value, axis, split_axis=0, concat_axis=0, tiled=True)  50.1 us
    all_to_all x2, blocking collectives, exchange(): return lax.all_to_all(value, axis, split_axis=0, concat_axis=0, tiled=True)  23.3 us
    all_gather x1, blocking collectives, sum_everywhere(): return lax.all_gather(whole, 'tm', axis=0, tiled=True).astype(jnp.float32)  16.4 us
    convert_element_type x1, other arithmetic, local_step(): (near_rows.astype(jnp.float32) + jnp.cos(phases)).astype(jnp.bfloat16)  10.1 us
    gather x1, local copies, waits for them, and re-layouts, local_step(): jnp.take(slot_rows, near_slots, axis=0)  7.57 us
  transfers between devices with their start and end apart: 6, of which 6 were waited for; matrix products, arithmetic and copies ran while one was open for 2% of the time, Pallas kernels for 0%

commit v1 on v0

--- a/solution.py
+++ b/solution.py
@@ -5,6 +5,11 @@
 from jax.sharding import PartitionSpec as P
 
 HEADS = 2
+
+
+def tiled_gather(x, axis, dim):
+    copies = jnp.concatenate([x] * lax.axis_size(axis), axis=dim)
+    return lax.all_to_all(copies, axis, dim, dim, tiled=True)
 
 
 def local_step(
@@ -83,7 +88,7 @@
     mine = jnp.sum(pieces.astype(jnp.float32), axis=0).astype(jnp.bfloat16)
     whole = exchange(jnp.broadcast_to(mine[None], (spots, cells, 128)), "dp")
     whole = whole.reshape(own, width)
-    return lax.all_gather(whole, "tm", axis=0, tiled=True).astype(jnp.float32)
+    return tiled_gather(whole, "tm", 0).astype(jnp.float32)
 
 
 def per_device(

time: 274 us -> 276 us (level)
  blocking collectives: 39.7 us -> 60.5 us
  waiting for transfers between devices: 142 us -> 123 us
  local copies, waits for them, and re-layouts: 14.5 us -> 18.2 us
  starting transfers between devices: 50.1 us -> 46.8 us
    all_to_all x2 -> x4, blocking collectives: 23.3 us -> 60.5 us  [exchange(): return lax.all_to_all(value, axis, split_axis=0, concat_axis=0, tiled=True)]
    all_to_all x6 -> x4, waiting for transfers between devices: 142 us -> 115 us  [exchange(): return lax.all_to_all(value, axis, split_axis=0, concat_axis=0, tiled=True)]
    all_gather x1 -> x0, blocking collectives: 16.4 us -> none  [sum_everywhere(): return lax.all_gather(whole, 'tm', axis=0, tiled=True).astype(jnp.float32)]
    all_to_all x6 -> x4, starting transfers between devices: 50.1 us -> 39.9 us  [exchange(): return lax.all_to_all(value, axis, split_axis=0, concat_axis=0, tiled=True)]
    all_to_all x0 -> x1, waiting for transfers between devices: none -> 7.35 us  [tiled_gather(): return lax.all_to_all(copies, axis, dim, dim, tiled=True)]
    all_to_all x0 -> x1, starting transfers between devices: none -> 6.92 us  [tiled_gather(): return lax.all_to_all(copies, axis, dim, dim, tiled=True)]
    unnamed x27 -> x34, local copies, waits for them, and re-layouts: 0.59 us -> 4.95 us
  transfers between devices with their start and end apart: 6 -> 5, of which waited for: 6 -> 5; matrix products, arithmetic and copies ran while one was open for 2% -> 2% of each run, Pallas kernels for 0% -> 0%
where the time goes in v1:
time: 276 us; the launch traced here: 275 us
  waiting for transfers between devices  123 us (45%)
  blocking collectives  60.5 us (22%)
  starting transfers between devices  46.8 us (17%)
  local copies, waits for them, and re-layouts  18.2 us (7%)
  other arithmetic  15.7 us (6%)
  matrix products  9.85 us (4%)
    all_to_all x4, waiting for transfers between devices, exchange(): return lax.all_to_all(value, axis, split_axis=0, concat_axis=0, tiled=True)  115 us
    all_to_all x4, blocking collectives, exchange(): return lax.all_to_all(value, axis, split_axis=0, concat_axis=0, tiled=True)  60.5 us
    all_to_all x4, starting transfers between devices, exchange(): return lax.all_to_all(value, axis, split_axis=0, concat_axis=0, tiled=True)  39.9 us
    convert_element_type x1, other arithmetic, local_step(): (near_rows.astype(jnp.float32) + jnp.cos(phases)).astype(jnp.bfloat16)  10.1 us
    gather x1, local copies, waits for them, and re-layouts, local_step(): jnp.take(slot_rows, near_slots, axis=0)  7.57 us
    all_to_all x1, waiting for transfers between devices, tiled_gather(): return lax.all_to_all(copies, axis, dim, dim, tiled=True)  7.35 us
    all_to_all x1, starting transfers between devices, tiled_gather(): return lax.all_to_all(copies, axis, dim, dim, tiled=True)  6.92 us
  transfers between devices with their start and end apart: 5, of which 5 were waited for; matrix products, arithmetic and copies ran while one was open for 2% of the time, Pallas kernels for 0%

profile of v1, /device:TPU:1, one launch (start us, length us, event | category | flops | bytes accessed | tf_op | source)
XLA Modules:
  0.0 274.8 jit_solution(8383268286700365743)
XLA Ops:
  2.4 1.4 reduce.7
  4.5 19.3 %all-to-all-start = ((s32[64,1,64]{2,1,0:T(1,128)}), s32[64,1,64]{2,1,0:T(1,128)S(1)}, u32[]{:S(2)}, u32[]{:S(2)}) async-start(s32[64,1,64]{2,1,0:T(1,128)} %bitcast.4), calls=%async_computation | async-start | bytes 65536 | tf_op jit(solution)/shard_map/all_to_all | solution.py:77
  23.8 2.6 convolution_convert_fusion
  26.3 10.8 %all-to-all-done = s32[64,1,64]{2,1,0:T(1,128)S(1)} async-done(((s32[64,1,64]{2,1,0:T(1,128)}), s32[64,1,64]{2,1,0:T(1,128)S(1)}, u32[]{:S(2)}, u32[]{:S(2)}) %all-to-all-start) | async-done | bytes 16416 | tf_op jit(solution)/shard_map/all_to_all | solution.py:77
  37.2 4.7 %all-to-all-start.1 = ((bf16[64,32,256]{2,1,0:T(8,128)(2,1)}), bf16[64,32,256]{2,1,0:T(8,128)(2,1)S(1)}, u32[]{:S(2)}, u32[]{:S(2)}) async-start(bf16[64,32,256]{2,1,0:T(8,128)(2,1)} %bitcast.8), calls=%async_computation.1 | async-start | bytes 2097152 | tf_op jit(solution)/shard_map/all_to_all | solution.py:77
  42.0 1.2 select_reduce_fusion
  43.3 48.9 %all-to-all-done.1 = bf16[64,32,256]{2,1,0:T(8,128)(2,1)S(1)} async-done(((bf16[64,32,256]{2,1,0:T(8,128)(2,1)}), bf16[64,32,256]{2,1,0:T(8,128)(2,1)S(1)}, u32[]{:S(2)}, u32[]{:S(2)}) %all-to-all-start.1) | async-done | bytes 1048608 | tf_op jit(solution)/shard_map/all_to_all | solution.py:77
  92.1 1.0 convolution_add_fusion.1
  93.8 10.3 %all-to-all-start.2 = ((bf16[8,32,256]{2,1,0:T(8,128)(2,1)}), bf16[8,32,256]{2,1,0:T(8,128)(2,1)S(1)}, u32[]{:S(2)}, u32[]{:S(2)}) async-start(bf16[8,32,256]{2,1,0:T(8,128)(2,1)} %pad_maximum_fusion.1), calls=%async_computation.2 | async-start | bytes 262144 | tf_op jit(solution)/shard_map/all_to_all | solution.py:77
  104.1 5.3 %all-to-all-done.2 = bf16[8,32,256]{2,1,0:T(8,128)(2,1)S(1)} async-done(((bf16[8,32,256]{2,1,0:T(8,128)(2,1)}), bf16[8,32,256]{2,1,0:T(8,128)(2,1)S(1)}, u32[]{:S(2)}, u32[]{:S(2)}) %all-to-all-start.2) | async-done | bytes 131104 | tf_op jit(solution)/shard_map/all_to_all | solution.py:77
  109.5 8.1 %all_to_all.56 = bf16[8,16,256]{2,1,0:T(8,128)(2,1)S(1)} all-to-all(bf16[8,16,256]{2,1,0:T(8,128)(2,1)S(1)} %constant_dynamic-update-slice_fusion), channel_id=1, replica_groups=mesh['tm'=8,'dp'=64] {'tm'}, dimensions={0} | all-to-all | bytes 131072 | tf_op jit(solution)/shard_map/all_to_all | solution.py:77
  117.6 1.5 convolution_convert_fusion.1
  119.1 5.7 %all-to-all-start.4 = ((bf16[64,32,256]{2,1,0:T(8,128)(2,1)}), bf16[64,32,256]{2,1,0:T(8,128)(2,1)S(1)}, u32[]{:S(2)}, u32[]{:S(2)}) async-start(bf16[64,32,256]{2,1,0:T(8,128)(2,1)} %bitcast.34), calls=%async_computation.4 | async-start | bytes 2097152 | tf_op jit(solution)/shard_map/all_to_all | solution.py:77
  126.0 50.3 %all-to-all-done.4 = bf16[64,32,256]{2,1,0:T(8,128)(2,1)S(1)} async-done(((bf16[64,32,256]{2,1,0:T(8,128)(2,1)}), bf16[64,32,256]{2,1,0:T(8,128)(2,1)S(1)}, u32[]{:S(2)}, u32[]{:S(2)}) %all-to-all-start.4) | async-done | bytes 1048608 | tf_op jit(solution)/shard_map/all_to_all | solution.py:77
  176.3 1.2 gather_fusion
  177.4 7.6 %gather_fusion.1 = bf16[2560,256]{1,0:T(8,128)(2,1)S(1)} fusion(bf16[2048,256]{1,0:T(8,128)(2,1)S(1)} %bitcast.275, s32[3072]{0:T(1024)S(1)} %pad_clamp_fusion), kind=kCustom, calls=%fused_computation.1 | custom fusion | bytes 2631680 | tf_op jit(solution)/shard_map/jit(_take)/gather | solution.py:31
  185.3 10.1 %add_convert_fusion = bf16[20,128,256]{2,1,0:T(8,128)(2,1)S(1)} fusion(f32[256]{0:T(256)S(1)} %copy-done.8, f32[20,128]{1,0:T(8,128)S(1)} %bitcast.293, bf16[20,128,256]{2,1,0:T(8,128)(2,1)S(1)} %bitcast.276, pred[20,128]{1,0:T(8,128)(4,1)S(1)} %compare_and_fusion), kind=kLoop, calls=%fused_computation.4 | loop fusion | flops 3276800 | bytes 2635264 | tf_op jit(solution)/shard_map/convert_element_type | solution.py:33
  196.2 1.1 multiply_reduce_fusion
  197.4 1.1 fusion.1
  200.4 15.2 %all_to_all.57 = bf16[8,96,256]{2,1,0:T(8,128)(2,1)S(1)} all-to-all(bf16[8,96,256]{2,1,0:T(8,128)(2,1)S(1)} %bitcast.277), channel_id=1, replica_groups=mesh['tm'=8,'dp'=64] {'tm'}, dimensions={0} | all-to-all | bytes 786432 | tf_op jit(solution)/shard_map/all_to_all | solution.py:77
  215.8 19.4 %all_to_all.58 = bf16[64,3,128]{2,1,0:T(4,128)(2,1)S(1)} all-to-all(bf16[64,3,128]{2,1,0:T(4,128)(2,1)S(1)} %reshape.234), channel_id=1, replica_groups=mesh['tm'=8,'dp'=64] {'dp'}, dimensions={0} | all-to-all | bytes 98304 | tf_op jit(solution)/shard_map/all_to_all | solution.py:77
  235.2 17.8 %all_to_all.59 = bf16[64,3,128]{2,1,0:T(4,128)(2,1)S(1)} all-to-all(bf16[64,3,128]{2,1,0:T(4,128)(2,1)S(1)} %broadcast_in_dim.73), channel_id=1, replica_groups=mesh['tm'=8,'dp'=64] {'dp'}, dimensions={0} | all-to-all | bytes 98304 | tf_op jit(solution)/shard_map/all_to_all | solution.py:77
  258.1 6.9 %all-to-all-start.8 = ((bf16[8,96,256]{2,1,0:T(8,128)(2,1)}), bf16[8,96,256]{2,1,0:T(8,128)(2,1)S(1)}, u32[]{:S(2)}, u32[]{:S(2)}) async-start(bf16[8,96,256]{2,1,0:T(8,128)(2,1)} %bitcast.79), calls=%async_computation.8 | async-start | bytes 786432 | tf_op jit(solution)/shard_map/all_to_all | solution.py:12
  265.8 7.3 %all-to-all-done.8 = bf16[8,96,256]{2,1,0:T(8,128)(2,1)S(1)} async-done(((bf16[8,96,256]{2,1,0:T(8,128)(2,1)}), bf16[8,96,256]{2,1,0:T(8,128)(2,1)S(1)}, u32[]{:S(2)}, u32[]{:S(2)}) %all-to-all-start.8) | async-done | bytes 393248 | tf_op jit(solution)/shard_map/all_to_all | solution.py:12
  (88 shorter events, 15.2 us)
Async XLA Ops:
  0.6 91.5 %copy-start = (bf16[256,512]{1,0:T(8,128)(2,1)S(1)}, bf16[256,512]{1,0:T(8,128)(2,1)}, u32[]{:S(2)}) copy-start(bf16[256,512]{1,0:T(8,128)(2,1)} %param.22) | copy-start | bytes 786436
  4.5 32.7 %all-to-all-start = ((s32[64,1,64]{2,1,0:T(1,128)}), s32[64,1,64]{2,1,0:T(1,128)S(1)}, u32[]{:S(2)}, u32[]{:S(2)}) async-start(s32[64,1,64]{2,1,0:T(1,128)} %bitcast.4), calls=%async_computation | async-start | bytes 65536 | tf_op jit(solution)/shard_map/all_to_all | solution.py:77
  26.3 65.8 %copy-start.9 = (f32[512]{0:T(512)S(1)}, f32[512]{0:T(512)}, u32[]{:S(2)}) copy-start(f32[512]{0:T(512)} %param.23) | copy-start | bytes 6148
  37.2 54.9 %all-to-all-start.1 = ((bf16[64,32,256]{2,1,0:T(8,128)(2,1)}), bf16[64,32,256]{2,1,0:T(8,128)(2,1)S(1)}, u32[]{:S(2)}, u32[]{:S(2)}) async-start(bf16[64,32,256]{2,1,0:T(8,128)(2,1)} %bitcast.8), calls=%async_computation.1 | async-start | bytes 2097152 | tf_op jit(solution)/shard_map/all_to_all | solution.py:77
  92.1 12.0 %copy-start.3 = (f32[128,256]{1,0:T(8,128)S(1)}, f32[128,256]{1,0:T(8,128)}, u32[]{:S(2)}) copy-start(f32[128,256]{1,0:T(8,128)} %param.20) | copy-start | bytes 393220
  93.8 15.5 %all-to-all-start.2 = ((bf16[8,32,256]{2,1,0:T(8,128)(2,1)}), bf16[8,32,256]{2,1,0:T(8,128)(2,1)S(1)}, u32[]{:S(2)}, u32[]{:S(2)}) async-start(bf16[8,32,256]{2,1,0:T(8,128)(2,1)} %pad_maximum_fusion.1), calls=%async_computation.2 | async-start | bytes 262144 | tf_op jit(solution)/shard_map/all_to_all | solution.py:77
  119.1 5.7 %copy-start.6 = (s32[1,20,128]{2,0,1:T(1,128)S(1)}, s32[1,20,128]{2,0,1:T(1,128)}, u32[]{:S(2)}) copy-start(s32[1,20,128]{2,0,1:T(1,128)} %param.17) | copy-start | bytes 30724
  119.1 5.8 %copy-start.2 = (bf16[4,256,256]{2,1,0:T(8,128)(2,1)S(1)}, bf16[4,256,256]{2,1,0:T(8,128)(2,1)}, u32[]{:S(2)}) copy-start(bf16[4,256,256]{2,1,0:T(8,128)(2,1)} %param.25) | copy-start | bytes 1572868
  119.1 57.2 %all-to-all-start.4 = ((bf16[64,32,256]{2,1,0:T(8,128)(2,1)}), bf16[64,32,256]{2,1,0:T(8,128)(2,1)S(1)}, u32[]{:S(2)}, u32[]{:S(2)}) async-start(bf16[64,32,256]{2,1,0:T(8,128)(2,1)} %bitcast.34), calls=%async_computation.4 | async-start | bytes 2097152 | tf_op jit(solution)/shard_map/all_to_all | solution.py:77
  124.8 1.1 copy-start.7
  124.8 1.1 copy-start.5
  177.4 7.9 %copy-start.8 = (f32[256]{0:T(256)S(1)}, f32[256]{0:T(256)}, u32[]{:S(2)}) copy-start(f32[256]{0:T(256)} %param.24) | copy-start | bytes 3076
  185.3 10.1 %copy-start.4 = (bf16[256,256]{1,0:T(8,128)(2,1)S(1)}, bf16[256,256]{1,0:T(8,128)(2,1)}, u32[]{:S(2)}) copy-start(bf16[256,256]{1,0:T(8,128)(2,1)} %copy.44) | copy-start | bytes 393220
  196.1 2.4 copy-start.1
  196.1 2.6 copy-start.10
  196.1 2.6 copy-start.11
  258.1 15.0 %all-to-all-start.8 = ((bf16[8,96,256]{2,1,0:T(8,128)(2,1)}), bf16[8,96,256]{2,1,0:T(8,128)(2,1)S(1)}, u32[]{:S(2)}, u32[]{:S(2)}) async-start(bf16[8,96,256]{2,1,0:T(8,128)(2,1)} %bitcast.79), calls=%async_computation.8 | async-start | bytes 786432 | tf_op jit(solution)/shard_map/all_to_all | solution.py:12
